TPU v7x, 256 devices: a whole 4x4x8 slice. The times are simulated.
256 devices in a mesh: dp: 4 (over x), seq: 64 (over z, y, core).
Axes of the slice: x: 4, y: 4, z: 8, core: 2. Of those that a mesh axis runs over, the one named last changes fastest.
Arguments:
- query_gate: bfloat16 [4, 8192, 4096], P('dp', 'seq'), may hold values from -6 to 6
- key_gate: bfloat16 [4, 8192, 4096], P('dp', 'seq'), may hold values from -6 to 6
- value_feat: bfloat16 [4, 8192, 4096], P('dp', 'seq'), may hold values from -6 to 6
- filters: bfloat16 [256, 128], replicated, may hold values from -0.5 to 0.5
- grad_out: bfloat16 [4, 8192, 4096], P('dp', 'seq'), may hold values from -6 to 6
- basis_prev: float32 [128, 16], replicated, may hold values from -6 to 6
Outputs:
- mixed_out: bfloat16 [4, 8192, 4096], P('dp', 'seq')
- grad_query: bfloat16 [4, 8192, 4096], P('dp', 'seq')
- grad_key: bfloat16 [4, 8192, 4096], P('dp', 'seq')
- grad_value: bfloat16 [4, 8192, 4096], P('dp', 'seq')
- low_rank_grad: float32 [256, 128], replicated
- basis_next: float32 [128, 16], replicated
All inputs are finite; a program needn't handle non-finite values.
Results may differ from a plain program's by a relative error of at most 0.0061.
Values may be sent and summed in bfloat16 or wider, within the bound.
No kernel may reach another device: no remote copies, remote signals or barrier semaphores. Data moves between devices by JAX's collectives and lax.ppermute only.
A program may use at most 192 MiB of HBM per device.

v0:
```python
import jax
import jax.numpy as jnp
from jax import lax
from jax.sharding import PartitionSpec as P


def shifted(block, axis, distance):
    devices = range(lax.axis_size(axis))
    route = [(i - distance, i) for i in devices if i - distance in devices]
    return lax.ppermute(block, axis, route)


def orthonormal(left):
    columns = []
    for index in range(left.shape[1]):
        column = left[:, index]
        if index > 0:
            basis = jnp.stack(columns, axis=1)
            coeffs = jnp.dot(basis.T, column, precision=lax.Precision.HIGHEST)
            column = column - jnp.dot(basis, coeffs, precision=lax.Precision.HIGHEST)
        columns.append(column / jnp.sqrt(jnp.sum(column * column) + 1e-06))
    return jnp.stack(columns, axis=1)


def banded(vec, rows):
    count, taps = vec.shape
    width = rows + taps - 1
    line = jnp.concatenate([vec, jnp.zeros((count, rows), vec.dtype)], axis=1)
    tiled = jnp.tile(line, (1, rows))[:, : rows * width]
    return tiled.reshape(count, rows, width)


def lag_sums(cross, taps):
    count, rows, width = cross.shape
    flat = cross.reshape(count, rows * width)[:, : (rows - 1) * 2 * taps]
    upper = flat.reshape(count, rows - 1, 2 * taps)[:, :, :taps].sum(axis=1)
    return upper + cross[:, rows - 1, rows - 1 : rows - 1 + taps]


def on_device(query_gate, key_gate, value_feat, filters, grad_out, basis_prev):
    gate_q = query_gate[0].astype(jnp.float32)
    gate_k = key_gate[0].astype(jnp.float32)
    feat_v = value_feat[0].astype(jnp.float32)
    cotan = grad_out[0].astype(jnp.float32)
    tok, channels = gate_q.shape
    groups, taps = filters.shape
    group_size = channels // groups
    width = tok + taps - 1
    product = (gate_k * feat_v).astype(jnp.bfloat16)
    grad_conv = (cotan * gate_q).astype(jnp.bfloat16)
    before = shifted(product[tok - (taps - 1) :], "seq", 1)
    after = shifted(grad_conv[: taps - 1], "seq", -1)
    prod_cm = jnp.concatenate([before, product], axis=0).T.reshape(groups, group_size, width)
    grad_cm = jnp.concatenate([grad_conv, after], axis=0).T.reshape(groups, group_size, width)
    block_groups = min(64, groups)
    conv_parts = []
    back_parts = []
    filter_parts = []
    for block in range(groups // block_groups):
        low = block * block_groups
        filt_blk = filters[low : low + block_groups]
        forward_tab = banded(filt_blk[:, ::-1], taps)
        backward_tab = banded(filt_blk, taps)
        prod_blk = prod_cm[low : low + block_groups]
        grad_blk = grad_cm[low : low + block_groups]
        conv_pos = jnp.einsum(
            "gcu,gsu->gcs", prod_blk, forward_tab, preferred_element_type=jnp.float32
        )
        back_pos = jnp.einsum(
            "gcu,gsu->gcs", grad_blk, backward_tab, preferred_element_type=jnp.float32
        )
        cross = jnp.einsum(
            "gcs,gcu->gsu", grad_blk[:, :, :taps], prod_blk, preferred_element_type=jnp.float32
        )
        lag_total = lag_sums(cross, taps)
        conv_parts.append(conv_pos)
        back_parts.append(back_pos)
        filter_parts.append(lag_total[:, ::-1])
    conv = jnp.concatenate(conv_parts, axis=0).reshape(channels, tok).T
    grad_product = jnp.concatenate(back_parts, axis=0).reshape(channels, tok).T
    local_grad = jnp.concatenate(filter_parts, axis=0)
    mixed_out = (gate_q * conv).astype(jnp.bfloat16)[None]
    grad_query = (cotan * conv).astype(jnp.bfloat16)[None]
    grad_key = (grad_product * feat_v).astype(jnp.bfloat16)[None]
    grad_value = (grad_product * gate_k).astype(jnp.bfloat16)[None]
    scale = (lax.axis_size("dp") * lax.axis_size("seq") * tok * group_size) ** (-0.5)
    seq_grad = lax.psum(local_grad, "seq")
    left = lax.psum(jnp.dot(seq_grad, basis_prev, precision=lax.Precision.HIGHEST), "dp")
    ortho = orthonormal(left)
    right = lax.psum(jnp.dot(seq_grad.T, ortho, precision=lax.Precision.HIGHEST), "dp")
    basis_next = right * scale
    low_rank_grad = jnp.dot(ortho, basis_next.T, precision=lax.Precision.HIGHEST)
    return (mixed_out, grad_query, grad_key, grad_value, low_rank_grad, basis_next)


def solution(mesh):
    return jax.shard_map(
        on_device,
        mesh=mesh,
        in_specs=(
            P("dp", "seq", None),
            P("dp", "seq", None),
            P("dp", "seq", None),
            P(),
            P("dp", "seq", None),
            P(),
        ),
        out_specs=(
            P("dp", "seq", None),
            P("dp", "seq", None),
            P("dp", "seq", None),
            P("dp", "seq", None),
            P(),
            P(),
        ),
        check_vma=False,
    )
```

profile of v0, /device:TPU:10, one launch (start us, length us, event | category | flops | bytes accessed | tf_op | source)
XLA Modules:
  0.0 581.4 jit_solution(8828656862283200973)
XLA Ops:
  16.9 16.3 %reshape.134 = bf16[64,128,255]{2,1,0:T(8,128)(2,1)} reshape(bf16[64,32640]{1,0:T(8,128)(2,1)} %slice.263) | data formatting | bytes 8355840 | tf_op jit(solution)/shard_map/reshape | solution.py:30
  38.3 15.8 %reshape.135 = bf16[64,128,255]{2,1,0:T(8,128)(2,1)} reshape(bf16[64,32640]{1,0:T(8,128)(2,1)} %slice.265) | data formatting | bytes 8355840 | tf_op jit(solution)/shard_map/reshape | solution.py:30
  59.2 16.0 %reshape.133 = bf16[64,128,255]{2,1,0:T(8,128)(2,1)} reshape(bf16[64,32640]{1,0:T(8,128)(2,1)} %slice.261) | data formatting | bytes 8355840 | tf_op jit(solution)/shard_map/reshape | solution.py:30
  80.3 15.8 %reshape.132 = bf16[64,128,255]{2,1,0:T(8,128)(2,1)} reshape(bf16[64,32640]{1,0:T(8,128)(2,1)} %slice.259) | data formatting | bytes 8355840 | tf_op jit(solution)/shard_map/reshape | solution.py:30
  97.4 3.6 fusion.64
  120.4 15.8 %reshape.129 = bf16[64,128,255]{2,1,0:T(8,128)(2,1)} reshape(bf16[64,32640]{1,0:T(8,128)(2,1)} %slice.254) | data formatting | bytes 8355840 | tf_op jit(solution)/shard_map/reshape | solution.py:30
  141.3 15.8 %reshape.130 = bf16[64,128,255]{2,1,0:T(8,128)(2,1)} reshape(bf16[64,32640]{1,0:T(8,128)(2,1)} %slice.256) | data formatting | bytes 8355840 | tf_op jit(solution)/shard_map/reshape | solution.py:30
  162.2 16.0 %reshape.128 = bf16[64,128,255]{2,1,0:T(8,128)(2,1)} reshape(bf16[64,32640]{1,0:T(8,128)(2,1)} %slice.252) | data formatting | bytes 8355840 | tf_op jit(solution)/shard_map/reshape | solution.py:30
  183.3 15.8 %reshape.127 = bf16[64,128,255]{2,1,0:T(8,128)(2,1)} reshape(bf16[64,32640]{1,0:T(8,128)(2,1)} %slice.250) | data formatting | bytes 8355840 | tf_op jit(solution)/shard_map/reshape | solution.py:30
  205.8 9.5 %reshape.139 = f32[64,32640]{1,0:T(8,128)} reshape(f32[64,128,255]{2,1,0:T(8,128)} %copy-done.1) | data formatting | bytes 16711680 | tf_op jit(solution)/shard_map/reshape | solution.py:35
  220.1 9.3 %reshape.141 = f32[64,32640]{1,0:T(8,128)} reshape(f32[64,128,255]{2,1,0:T(8,128)} %copy-done.2) | data formatting | bytes 16711680 | tf_op jit(solution)/shard_map/reshape | solution.py:35
  234.3 9.3 %reshape.143 = f32[64,32640]{1,0:T(8,128)} reshape(f32[64,128,255]{2,1,0:T(8,128)} %copy-done.3) | data formatting | bytes 16711680 | tf_op jit(solution)/shard_map/reshape | solution.py:35
  248.5 9.3 %reshape.137 = f32[64,32640]{1,0:T(8,128)} reshape(f32[64,128,255]{2,1,0:T(8,128)} %copy-done.4) | data formatting | bytes 16711680 | tf_op jit(solution)/shard_map/reshape | solution.py:35
  270.7 7.1 %slice.271 = f32[64,32512]{1,0:T(8,128)} slice(f32[64,32640]{1,0:T(8,128)} %reshape.139), slice={[0:64], [0:32512]} | slice | bytes 16646144 | tf_op jit(solution)/shard_map/slice | solution.py:35
  277.8 7.7 %reshape.140 = f32[64,127,256]{2,1,0:T(8,128)} reshape(f32[64,32512]{1,0:T(8,128)} %slice.271) | data formatting | bytes 16646144 | tf_op jit(solution)/shard_map/reshape | solution.py:36
  288.2 7.1 %slice.275 = f32[64,32512]{1,0:T(8,128)} slice(f32[64,32640]{1,0:T(8,128)} %reshape.141), slice={[0:64], [0:32512]} | slice | bytes 16646144 | tf_op jit(solution)/shard_map/slice | solution.py:35
  295.3 7.4 %reshape.142 = f32[64,127,256]{2,1,0:T(8,128)} reshape(f32[64,32512]{1,0:T(8,128)} %slice.275) | data formatting | bytes 16646144 | tf_op jit(solution)/shard_map/reshape | solution.py:36
  305.4 7.1 %slice.279 = f32[64,32512]{1,0:T(8,128)} slice(f32[64,32640]{1,0:T(8,128)} %reshape.143), slice={[0:64], [0:32512]} | slice | bytes 16646144 | tf_op jit(solution)/shard_map/slice | solution.py:35
  312.5 7.4 %reshape.144 = f32[64,127,256]{2,1,0:T(8,128)} reshape(f32[64,32512]{1,0:T(8,128)} %slice.279) | data formatting | bytes 16646144 | tf_op jit(solution)/shard_map/reshape | solution.py:36
  322.7 7.1 %slice.267 = f32[64,32512]{1,0:T(8,128)} slice(f32[64,32640]{1,0:T(8,128)} %reshape.137), slice={[0:64], [0:32512]} | slice | bytes 16646144 | tf_op jit(solution)/shard_map/slice | solution.py:35
  329.8 7.4 %reshape.138 = f32[64,127,256]{2,1,0:T(8,128)} reshape(f32[64,32512]{1,0:T(8,128)} %slice.267) | data formatting | bytes 16646144 | tf_op jit(solution)/shard_map/reshape | solution.py:36
  343.8 174.6 %all-reduce.10.cloned.1.call-done = f32[256,128]{1,0:T(8,128)} async-done(((f32[256,128]{1,0:T(8,128)}), f32[256,128]{1,0:T(8,128)}) %all-reduce.10.cloned.1.call-update) | async-done | bytes 131088 | tf_op jit(solution)/shard_map/psum | solution.py:87
  519.5 13.9 %psum.22 = f32[256,16]{0,1:T(8,128)S(1)} all-reduce(f32[256,16]{0,1:T(8,128)S(1)} %fusion.66), channel_id=1, replica_groups=mesh['dp'=4,'seq'=64] {'dp'}, use_global_device_ids=true, to_apply=%region_5.0 | all-reduce | flops 4096 | bytes 32768 | tf_op jit(solution)/shard_map/psum | solution.py:88
  561.9 11.3 %psum.23 = f32[128,16]{0,1:T(8,128)S(1)} all-reduce(f32[128,16]{0,1:T(8,128)S(1)} %fusion.78), channel_id=1, replica_groups=mesh['dp'=4,'seq'=64] {'dp'}, use_global_device_ids=true, to_apply=%region_22.0 | all-reduce | flops 2048 | bytes 16384 | tf_op jit(solution)/shard_map/psum | solution.py:90
  (208 shorter events, 128.7 us)
Async XLA Ops:
  7.2 511.2 %copy-start = (f32[128,16]{0,1:T(8,128)S(1)}, f32[128,16]{0,1:T(8,128)}, u32[]{:S(2)}) copy-start(f32[128,16]{0,1:T(8,128)} %param.11) | copy-start | bytes 24580
  7.2 511.2 %all-reduce.10.cloned.1.call-start = ((), (), s32[]{:S(2)}) async-start(), calls=%async_computation | async-start | bytes 262144 | tf_op jit(solution)/shard_map/psum | solution.py:87
  9.0 87.1 %collective-permute-start.1 = (bf16[127,4096]{1,0:T(8,128)(2,1)S(1)}, bf16[127,4096]{1,0:T(8,128)(2,1)S(1)}, u32[]{:S(2)}, u32[]{:S(2)}) collective-permute-start(bf16[127,4096]{1,0:T(8,128)(2,1)S(1)} %bitcast.286), channel_id=1, source_target_pairs={{1,0},{2,1},{3,2},{4,3},{5,4},{6,5},{7,6},{8,7},{9,8},{10,9},{11,1... | collective-permute-start | bytes 3121160 | tf_op jit(solution)/shard_map/ppermute | solution.py:10
  96.7 6.7 %copy-start.11 = (bf16[1024,255]{1,0:T(8,128)(2,1)}, bf16[1024,255]{1,0:T(8,128)(2,1)S(1)}, u32[]{:S(2)}) copy-start(bf16[1024,255]{1,0:T(8,128)(2,1)S(1)} %copy.30) | copy-start | bytes 1566724
  96.9 5.3 copy-start.13
  97.1 5.1 copy-start.15
  97.3 4.9 copy-start.17
  97.4 3.6 copy-start.7
  97.4 4.9 copy-start.8
  101.0 2.7 copy-start.9
  112.5 86.5 %collective-permute-start = (bf16[127,4096]{1,0:T(8,128)(2,1)S(1)}, bf16[127,4096]{1,0:T(8,128)(2,1)}, u32[]{:S(2)}, u32[]{:S(2)}) collective-permute-start(bf16[127,4096]{1,0:T(8,128)(2,1)S(1)} %slice.248), channel_id=1, source_target_pairs={{0,1},{1,2},{2,3},{3,4},{4,5},{5,6},{6,7},{7,8},{8,9},{9,10},{10,1... | collective-permute-start | bytes 3121160 | tf_op jit(solution)/shard_map/ppermute | solution.py:10
  199.1 2.0 copy-start.18
  202.4 3.2 copy-start.1
  205.8 9.7 %copy-start.16 = (bf16[1024,255]{1,0:T(8,128)(2,1)S(1)}, bf16[1024,255]{1,0:T(8,128)(2,1)}, u32[]{:S(2)}) copy-start(bf16[1024,255]{1,0:T(8,128)(2,1)} %copy-done.15) | copy-start | bytes 1566724
  216.8 3.2 copy-start.2
  220.1 9.5 %copy-start.14 = (bf16[1024,255]{1,0:T(8,128)(2,1)S(1)}, bf16[1024,255]{1,0:T(8,128)(2,1)}, u32[]{:S(2)}) copy-start(bf16[1024,255]{1,0:T(8,128)(2,1)} %copy-done.13) | copy-start | bytes 1566724
  230.9 3.2 copy-start.3
  234.3 9.5 %copy-start.12 = (bf16[1024,255]{1,0:T(8,128)(2,1)S(1)}, bf16[1024,255]{1,0:T(8,128)(2,1)}, u32[]{:S(2)}) copy-start(bf16[1024,255]{1,0:T(8,128)(2,1)} %copy-done.11) | copy-start | bytes 1566724
  245.1 3.2 copy-start.4
  257.8 7.1 %copy-start.5 = (bf16[64,128,255]{2,1,0:T(8,128)(2,1)S(1)}, bf16[64,128,255]{2,1,0:T(8,128)(2,1)}, u32[]{:S(2)}) copy-start(bf16[64,128,255]{2,1,0:T(8,128)(2,1)} %reshape.129) | copy-start | bytes 12533764
  261.3 4.8 copy-start.6
  337.2 3.5 copy-start.10
  573.2 1.1 copy-start.19
Sparse Core Ops, SparseCore 0:
  340.9 177.4 all-reduce.9
where the time goes:
time: 586 us; the launch traced here: 581 us
  local copies, waits for them, and re-layouts  286 us (49%)
  waiting for transfers between devices  175 us (30%)
  other arithmetic  36.3 us (6%)
  matrix products  28.7 us (5%)
  between operations  26.1 us (4%)
  blocking collectives  25.2 us (4%)
    psum x1, waiting for transfers between devices, on_device(): seq_grad = lax.psum(local_grad, 'seq')  175 us
    reshape x8, local copies, waits for them, and re-layouts, banded(): return tiled.reshape(count, rows, width)  127 us
    reshape x4, local copies, waits for them, and re-layouts, lag_sums(): flat = cross.reshape(count, rows * width)[:, :(rows - 1) * 2 * taps]  37.3 us
    unnamed x48, local copies, waits for them, and re-layouts  33.8 us
    reshape x4, local copies, waits for them, and re-layouts, lag_sums(): upper = flat.reshape(count, rows - 1, 2 * taps)[:, :, :taps].sum(axis=1)  30 us
    slice x4, local copies, waits for them, and re-layouts, lag_sums(): flat = cross.reshape(count, rows * width)[:, :(rows - 1) * 2 * taps]  28.4 us
    slice x8, local copies, waits for them, and re-layouts, banded(): tiled = jnp.tile(line, (1, rows))[:, :rows * width]  17.7 us
    psum x1, blocking collectives, on_device(): lax.psum(jnp.dot(seq_grad, basis_prev, precision=lax.Precision.HIGHEST),...  13.9 us
  transfers between devices with their start and end apart: 3, of which 1 were waited for; matrix products, arithmetic and copies ran while one was open for 30% of the time, Pallas kernels for 0%

commit v1 on v0

--- a/solution.py
+++ b/solution.py
@@ -84,7 +84,7 @@
     grad_key = (grad_product * feat_v).astype(jnp.bfloat16)[None]
     grad_value = (grad_product * gate_k).astype(jnp.bfloat16)[None]
     scale = (lax.axis_size("dp") * lax.axis_size("seq") * tok * group_size) ** (-0.5)
-    seq_grad = lax.psum(local_grad, "seq")
+    seq_grad = jnp.sum(lax.all_gather(local_grad, "seq"), axis=0)
     left = lax.psum(jnp.dot(seq_grad, basis_prev, precision=lax.Precision.HIGHEST), "dp")
     ortho = orthonormal(left)
     right = lax.psum(jnp.dot(seq_grad.T, ortho, precision=lax.Precision.HIGHEST), "dp")

time: 586 us -> 433 us (0.74)
  the two profiles are of different devices: /device:TPU:10 before, /device:TPU:130 now
where the time goes in v1:
time: 433 us; the launch traced here: 429 us
  local copies, waits for them, and re-layouts  288 us (67%)
  other arithmetic  38.8 us (9%)
  matrix products  26.9 us (6%)
  between operations  26.1 us (6%)
  blocking collectives  25.3 us (6%)
  waiting for transfers between devices  17.5 us (4%)
  starting transfers between devices  6 us (1%)
    reshape x8, local copies, waits for them, and re-layouts, banded(): return tiled.reshape(count, rows, width)  128 us
    reshape x4, local copies, waits for them, and re-layouts, lag_sums(): flat = cross.reshape(count, rows * width)[:, :(rows - 1) * 2 * taps]  37.1 us
    unnamed x42, local copies, waits for them, and re-layouts  33.8 us
    reshape x4, local copies, waits for them, and re-layouts, lag_sums(): upper = flat.reshape(count, rows - 1, 2 * taps)[:, :, :taps].sum(axis=1)  30.1 us
    slice x4, local copies, waits for them, and re-layouts, lag_sums(): flat = cross.reshape(count, rows * width)[:, :(rows - 1) * 2 * taps]  28.4 us
    slice x8, local copies, waits for them, and re-layouts, banded(): tiled = jnp.tile(line, (1, rows))[:, :rows * width]  17.8 us
    ppermute x2, waiting for transfers between devices, shifted(): return lax.ppermute(block, axis, route)  17.5 us
    psum x1, blocking collectives, on_device(): lax.psum(jnp.dot(seq_grad, basis_prev, precision=lax.Precision.HIGHEST),...  14 us
  transfers between devices with their start and end apart: 3, of which 1 were waited for; matrix products, arithmetic and copies ran while one was open for 43% of the time, Pallas kernels for 0%

profile of v1, /device:TPU:130, one launch (start us, length us, event | category | flops | bytes accessed | tf_op | source)
XLA Modules:
  0.0 428.5 jit_solution(4786786200335548332)
XLA Ops:
  9.0 3.9 collective-permute-start.1
  18.9 16.3 %reshape.134 = bf16[64,128,255]{2,1,0:T(8,128)(2,1)} reshape(bf16[64,32640]{1,0:T(8,128)(2,1)} %slice.263) | data formatting | bytes 8355840 | tf_op jit(solution)/shard_map/reshape | solution.py:30
  40.3 15.8 %reshape.135 = bf16[64,128,255]{2,1,0:T(8,128)(2,1)} reshape(bf16[64,32640]{1,0:T(8,128)(2,1)} %slice.265) | data formatting | bytes 8355840 | tf_op jit(solution)/shard_map/reshape | solution.py:30
  61.2 16.0 %reshape.133 = bf16[64,128,255]{2,1,0:T(8,128)(2,1)} reshape(bf16[64,32640]{1,0:T(8,128)(2,1)} %slice.261) | data formatting | bytes 8355840 | tf_op jit(solution)/shard_map/reshape | solution.py:30
  82.2 15.8 %reshape.132 = bf16[64,128,255]{2,1,0:T(8,128)(2,1)} reshape(bf16[64,32640]{1,0:T(8,128)(2,1)} %slice.259) | data formatting | bytes 8355840 | tf_op jit(solution)/shard_map/reshape | solution.py:30
  116.3 17.5 %collective-permute-done = bf16[127,4096]{1,0:T(8,128)(2,1)S(1)} collective-permute-done((bf16[127,4096]{1,0:T(8,128)(2,1)S(1)}, bf16[127,4096]{1,0:T(8,128)(2,1)S(1)}, u32[]{:S(2)}, u32[]{:S(2)}) %collective-permute-start) | collective-permute-done | bytes 1040416 | tf_op jit(solution)/shard_map/ppermute | solution.py:10
  140.2 9.3 %reshape.139 = f32[64,32640]{1,0:T(8,128)} reshape(f32[64,128,255]{2,1,0:T(8,128)} %copy-done.1) | data formatting | bytes 16711680 | tf_op jit(solution)/shard_map/reshape | solution.py:35
  155.4 9.2 %reshape.141 = f32[64,32640]{1,0:T(8,128)} reshape(f32[64,128,255]{2,1,0:T(8,128)} %copy-done.2) | data formatting | bytes 16711680 | tf_op jit(solution)/shard_map/reshape | solution.py:35
  169.5 9.3 %reshape.143 = f32[64,32640]{1,0:T(8,128)} reshape(f32[64,128,255]{2,1,0:T(8,128)} %copy-done.3) | data formatting | bytes 16711680 | tf_op jit(solution)/shard_map/reshape | solution.py:35
  183.7 9.3 %reshape.137 = f32[64,32640]{1,0:T(8,128)} reshape(f32[64,128,255]{2,1,0:T(8,128)} %copy-done.4) | data formatting | bytes 16711680 | tf_op jit(solution)/shard_map/reshape | solution.py:35
  192.9 7.1 %slice.271 = f32[64,32512]{1,0:T(8,128)} slice(f32[64,32640]{1,0:T(8,128)} %reshape.139), slice={[0:64], [0:32512]} | slice | bytes 16646144 | tf_op jit(solution)/shard_map/slice | solution.py:35
  200.0 7.4 %reshape.140 = f32[64,127,256]{2,1,0:T(8,128)} reshape(f32[64,32512]{1,0:T(8,128)} %slice.271) | data formatting | bytes 16646144 | tf_op jit(solution)/shard_map/reshape | solution.py:36
  210.2 7.1 %slice.275 = f32[64,32512]{1,0:T(8,128)} slice(f32[64,32640]{1,0:T(8,128)} %reshape.141), slice={[0:64], [0:32512]} | slice | bytes 16646144 | tf_op jit(solution)/shard_map/slice | solution.py:35
  217.3 7.8 %reshape.142 = f32[64,127,256]{2,1,0:T(8,128)} reshape(f32[64,32512]{1,0:T(8,128)} %slice.275) | data formatting | bytes 16646144 | tf_op jit(solution)/shard_map/reshape | solution.py:36
  227.8 7.1 %slice.279 = f32[64,32512]{1,0:T(8,128)} slice(f32[64,32640]{1,0:T(8,128)} %reshape.143), slice={[0:64], [0:32512]} | slice | bytes 16646144 | tf_op jit(solution)/shard_map/slice | solution.py:35
  234.9 7.4 %reshape.144 = f32[64,127,256]{2,1,0:T(8,128)} reshape(f32[64,32512]{1,0:T(8,128)} %slice.279) | data formatting | bytes 16646144 | tf_op jit(solution)/shard_map/reshape | solution.py:36
  245.1 7.1 %slice.267 = f32[64,32512]{1,0:T(8,128)} slice(f32[64,32640]{1,0:T(8,128)} %reshape.137), slice={[0:64], [0:32512]} | slice | bytes 16646144 | tf_op jit(solution)/shard_map/slice | solution.py:35
  252.2 7.4 %reshape.138 = f32[64,127,256]{2,1,0:T(8,128)} reshape(f32[64,32512]{1,0:T(8,128)} %slice.267) | data formatting | bytes 16646144 | tf_op jit(solution)/shard_map/reshape | solution.py:36
  268.6 16.0 %reshape.129 = bf16[64,128,255]{2,1,0:T(8,128)(2,1)} reshape(bf16[64,32640]{1,0:T(8,128)(2,1)} %slice.254) | data formatting | bytes 8355840 | tf_op jit(solution)/shard_map/reshape | solution.py:30
  289.6 15.9 %reshape.130 = bf16[64,128,255]{2,1,0:T(8,128)(2,1)} reshape(bf16[64,32640]{1,0:T(8,128)(2,1)} %slice.256) | data formatting | bytes 8355840 | tf_op jit(solution)/shard_map/reshape | solution.py:30
  310.6 16.0 %reshape.128 = bf16[64,128,255]{2,1,0:T(8,128)(2,1)} reshape(bf16[64,32640]{1,0:T(8,128)(2,1)} %slice.252) | data formatting | bytes 8355840 | tf_op jit(solution)/shard_map/reshape | solution.py:30
  331.7 15.8 %reshape.127 = bf16[64,128,255]{2,1,0:T(8,128)(2,1)} reshape(bf16[64,32640]{1,0:T(8,128)(2,1)} %slice.250) | data formatting | bytes 8355840 | tf_op jit(solution)/shard_map/reshape | solution.py:30
  367.5 14.0 %psum.14 = f32[256,16]{0,1:T(8,128)S(1)} all-reduce(f32[256,16]{0,1:T(8,128)S(1)} %fusion.66), channel_id=1, replica_groups=mesh['dp'=4,'seq'=64] {'dp'}, use_global_device_ids=true, to_apply=%region_5.0 | all-reduce | flops 4096 | bytes 32768 | tf_op jit(solution)/shard_map/psum | solution.py:88
  409.1 11.3 %psum.15 = f32[128,16]{0,1:T(8,128)S(1)} all-reduce(f32[128,16]{0,1:T(8,128)S(1)} %fusion.78), channel_id=1, replica_groups=mesh['dp'=4,'seq'=64] {'dp'}, use_global_device_ids=true, to_apply=%region_22.0 | all-reduce | flops 2048 | bytes 16384 | tf_op jit(solution)/shard_map/psum | solution.py:90
  (203 shorter events, 132.6 us)
Async XLA Ops:
  7.2 360.2 %copy-start = (f32[128,16]{0,1:T(8,128)S(1)}, f32[128,16]{0,1:T(8,128)}, u32[]{:S(2)}) copy-start(f32[128,16]{0,1:T(8,128)} %param.11) | copy-start | bytes 24580
  7.2 356.4 %all-gather.3.cloned.1.call-start = ((), (), s32[]{:S(2)}) async-start(), calls=%async_computation | async-start | bytes 8519680 | tf_op jit(solution)/shard_map/all_gather | solution.py:87
  9.0 89.0 %collective-permute-start.1 = (bf16[127,4096]{1,0:T(8,128)(2,1)S(1)}, bf16[127,4096]{1,0:T(8,128)(2,1)S(1)}, u32[]{:S(2)}, u32[]{:S(2)}) collective-permute-start(bf16[127,4096]{1,0:T(8,128)(2,1)S(1)} %bitcast.288), channel_id=1, source_target_pairs={{1,0},{2,1},{3,2},{4,3},{5,4},{6,5},{7,6},{8,7},{9,8},{10,9},{11,1... | collective-permute-start | bytes 3121160 | tf_op jit(solution)/shard_map/ppermute | solution.py:10
  99.0 5.0 %copy-start.11 = (bf16[1024,255]{1,0:T(8,128)(2,1)}, bf16[1024,255]{1,0:T(8,128)(2,1)S(1)}, u32[]{:S(2)}) copy-start(bf16[1024,255]{1,0:T(8,128)(2,1)S(1)} %copy.32) | copy-start | bytes 1566724
  99.2 4.8 %copy-start.13 = (bf16[1024,255]{1,0:T(8,128)(2,1)}, bf16[1024,255]{1,0:T(8,128)(2,1)S(1)}, u32[]{:S(2)}) copy-start(bf16[1024,255]{1,0:T(8,128)(2,1)S(1)} %copy.31) | copy-start | bytes 1566724
  99.2 3.6 copy-start.5
  99.3 4.9 %copy-start.6 = (bf16[64,128,255]{2,1,0:T(8,128)(2,1)S(1)}, bf16[64,128,255]{2,1,0:T(8,128)(2,1)}, u32[]{:S(2)}) copy-start(bf16[64,128,255]{2,1,0:T(8,128)(2,1)} %reshape.133) | copy-start | bytes 12533764
  102.9 2.7 copy-start.8
  114.2 21.3 %copy-start.14 = (bf16[1024,255]{1,0:T(8,128)(2,1)S(1)}, bf16[1024,255]{1,0:T(8,128)(2,1)}, u32[]{:S(2)}) copy-start(bf16[1024,255]{1,0:T(8,128)(2,1)} %copy-done.13) | copy-start | bytes 1566724
  114.2 19.6 %collective-permute-start = (bf16[127,4096]{1,0:T(8,128)(2,1)S(1)}, bf16[127,4096]{1,0:T(8,128)(2,1)S(1)}, u32[]{:S(2)}, u32[]{:S(2)}) collective-permute-start(bf16[127,4096]{1,0:T(8,128)(2,1)S(1)} %slice.248), channel_id=1, source_target_pairs={{0,1},{1,2},{2,3},{3,4},{4,5},{5,6},{6,7},{7,8},{8,9},{9,10},{10,1... | collective-permute-start | bytes 3121160 | tf_op jit(solution)/shard_map/ppermute | solution.py:10
  136.8 3.2 copy-start.1
  140.2 10.5 %copy-start.12 = (bf16[1024,255]{1,0:T(8,128)(2,1)S(1)}, bf16[1024,255]{1,0:T(8,128)(2,1)}, u32[]{:S(2)}) copy-start(bf16[1024,255]{1,0:T(8,128)(2,1)} %copy-done.11) | copy-start | bytes 1566724
  152.0 3.2 copy-start.2
  166.1 3.2 copy-start.3
  169.5 9.3 %copy-start.15 = (bf16[1024,255]{0,1:T(8,128)(2,1)S(1)}, bf16[1024,255]{0,1:T(8,128)(2,1)}, u32[]{:S(2)}) copy-start(bf16[1024,255]{0,1:T(8,128)(2,1)} %get-tuple-element.43) | copy-start | bytes 1566724
  180.3 3.2 copy-start.4
  347.5 7.1 %copy-start.7 = (bf16[64,128,255]{2,1,0:T(8,128)(2,1)S(1)}, bf16[64,128,255]{2,1,0:T(8,128)(2,1)}, u32[]{:S(2)}) copy-start(bf16[64,128,255]{2,1,0:T(8,128)(2,1)} %reshape.129) | copy-start | bytes 12533764
  351.0 4.8 %copy-start.9 = (bf16[64,128,255]{2,1,0:T(8,128)(2,1)S(1)}, bf16[64,128,255]{2,1,0:T(8,128)(2,1)}, u32[]{:S(2)}) copy-start(bf16[64,128,255]{2,1,0:T(8,128)(2,1)} %reshape.128) | copy-start | bytes 12533764
  357.0 3.5 copy-start.10
  420.4 1.1 copy-start.16
Sparse Core Ops, SparseCore 0:
  263.2 79.0 all-gather.2
